TPU v7x, 32 devices: a whole 2x2x4 slice. The times are simulated.
32 devices in a mesh: frame: 16 (over z, x, core), head: 2 (over y).
Axes of the slice: x: 2, y: 2, z: 4, core: 2. Of those that a mesh axis runs over, the one named last changes fastest.
Arguments:
- activations: bfloat16 [32, 128, 4096], P('frame'), may hold values from -6 to 6
- w_query: bfloat16 [4096, 4096], P('frame', 'head'), may hold values from -0.09375 to 0.09375
- w_key: bfloat16 [4096, 4096], P('frame', 'head'), may hold values from -0.09375 to 0.09375
- w_value: bfloat16 [4096, 4096], P('frame', 'head'), may hold values from -0.09375 to 0.09375
- q_gain: float32 [128], replicated, may hold values from 0.1 to 1.9
- k_gain: float32 [128], replicated, may hold values from 0.1 to 1.9
- grad_attn: bfloat16 [32, 128, 4096], P('frame', None, 'head'), may hold values from -6 to 6
Outputs:
- grad_input: bfloat16 [32, 128, 4096], P('frame', None, 'head')
- grad_wq: float32 [4096, 4096], P('frame', 'head')
- grad_wk: float32 [4096, 4096], P('frame', 'head')
- grad_wv: float32 [4096, 4096], P('frame', 'head')
All inputs are finite; a program needn't handle non-finite values.
Results may differ from a plain program's by a relative error of at most 0.018.
Values may be sent and summed in bfloat16 or wider, within the bound.
A program may use at most 192 MiB of HBM per device.

v0:
```python
import math

import jax
import jax.numpy as jnp
from jax import lax
from jax.sharding import PartitionSpec as P

HD = 128


epsilon = 1e-06


def scaled(raw, gain):
    inverse = lax.rsqrt(jnp.mean(raw * raw, axis=-1, keepdims=True) + epsilon)
    return raw * inverse * gain


def attend(query, key_norm, value):
    factor = 1.0 / math.sqrt(query.shape[-1])
    scores = jnp.einsum("fphd,gphd->phfg", query, key_norm) * factor
    expon = jnp.exp(scores)
    weights = expon / jnp.sum(expon, axis=-1, keepdims=True)
    return jnp.einsum("phfg,gphd->fphd", weights, value)


def attend_back(query, key_norm, value, cotan):
    _, pull = jax.vjp(
        attend, query.astype(jnp.float32), key_norm.astype(jnp.float32), value.astype(jnp.float32)
    )
    grads = pull(cotan.astype(jnp.float32))
    return (
        grads[0].astype(jnp.bfloat16),
        grads[1].astype(jnp.bfloat16),
        grads[2].astype(jnp.bfloat16),
    )


def body(activations, w_query, w_key, w_value, q_gain, k_gain, grad_attn):
    frames_here, patches, width = activations.shape
    head_cols = w_query.shape[1]
    heads_here = head_cols // HD
    count_rows = frames_here * patches
    full_query, full_key, full_value = (
        lax.all_gather(w_query, "frame", axis=0, tiled=True),
        lax.all_gather(w_key, "frame", axis=0, tiled=True),
        lax.all_gather(w_value, "frame", axis=0, tiled=True),
    )
    tok_rows = activations.reshape(count_rows, width)
    q_raw = jnp.dot(tok_rows, full_query, preferred_element_type=jnp.float32).reshape(
        count_rows, heads_here, HD
    )
    k_raw = jnp.dot(tok_rows, full_key, preferred_element_type=jnp.float32).reshape(
        count_rows, heads_here, HD
    )
    shape4 = (frames_here, patches, heads_here, HD)
    q_norm = scaled(q_raw, q_gain).astype(jnp.bfloat16).reshape(shape4)
    k_norm = scaled(k_raw, k_gain).astype(jnp.bfloat16).reshape(shape4)
    value = (
        jnp.dot(tok_rows, full_value, preferred_element_type=jnp.float32)
        .astype(jnp.bfloat16)
        .reshape(shape4)
    )
    cotan = grad_attn.reshape(shape4)
    moved = (
        lax.all_to_all(q_norm, "frame", split_axis=1, concat_axis=0, tiled=True),
        lax.all_to_all(k_norm, "frame", split_axis=1, concat_axis=0, tiled=True),
        lax.all_to_all(value, "frame", split_axis=1, concat_axis=0, tiled=True),
        lax.all_to_all(cotan, "frame", split_axis=1, concat_axis=0, tiled=True),
    )
    grads = attend_back(moved[0], moved[1], moved[2], moved[3])
    d_qn, d_kn, d_val = (
        lax.all_to_all(grads[0], "frame", split_axis=0, concat_axis=1, tiled=True),
        lax.all_to_all(grads[1], "frame", split_axis=0, concat_axis=1, tiled=True),
        lax.all_to_all(grads[2], "frame", split_axis=0, concat_axis=1, tiled=True),
    )
    _, pull_query = jax.vjp(lambda raw: scaled(raw, q_gain), q_raw)
    _, pull_key = jax.vjp(lambda raw: scaled(raw, k_gain), k_raw)
    d_q_raw = pull_query(d_qn.reshape(count_rows, heads_here, HD).astype(jnp.float32))[0]
    d_q_raw = d_q_raw.astype(jnp.bfloat16).reshape(count_rows, head_cols)
    d_k_raw = pull_key(d_kn.reshape(count_rows, heads_here, HD).astype(jnp.float32))[0]
    d_k_raw = d_k_raw.astype(jnp.bfloat16).reshape(count_rows, head_cols)
    d_v_rows = d_val.reshape(count_rows, head_cols)
    contract = (((1,), (1,)), ((), ()))
    partial_sum = lax.dot_general(d_q_raw, full_query, contract, preferred_element_type=jnp.float32)
    partial_sum = partial_sum + lax.dot_general(
        d_k_raw, full_key, contract, preferred_element_type=jnp.float32
    )
    partial_sum = partial_sum + lax.dot_general(
        d_v_rows, full_value, contract, preferred_element_type=jnp.float32
    )
    grad_input = lax.psum_scatter(
        partial_sum.reshape(frames_here, patches, width).astype(jnp.bfloat16),
        "head",
        scatter_dimension=2,
        tiled=True,
    )
    d_all = jnp.concatenate([d_q_raw, d_k_raw, d_v_rows], axis=1)
    over_tokens = (((0,), (0,)), ((), ()))
    term = lax.dot_general(tok_rows, d_all, over_tokens, preferred_element_type=jnp.float32)
    summed = lax.psum_scatter(
        term.astype(jnp.bfloat16), "frame", scatter_dimension=0, tiled=True
    ).astype(jnp.float32)
    grad_wq = summed[:, :head_cols]
    grad_wk = summed[:, head_cols : 2 * head_cols]
    grad_wv = summed[:, 2 * head_cols :]
    return (grad_input, grad_wq, grad_wk, grad_wv)


def solution(mesh):
    placed = (
        P("frame", None, None),
        P("frame", "head"),
        P("frame", "head"),
        P("frame", "head"),
        P(),
        P(),
        P("frame", None, "head"),
    )
    return jax.shard_map(
        body,
        mesh=mesh,
        in_specs=placed,
        out_specs=(
            P("frame", None, "head"),
            P("frame", "head"),
            P("frame", "head"),
            P("frame", "head"),
        ),
        check_vma=False,
    )
```

profile of v0, /device:TPU:0, one launch (start us, length us, event | category | flops | bytes accessed | tf_op | source)
XLA Modules:
  0.0 1106.9 jit_solution(1062887460003458384)
XLA Ops:
  10.8 7.4 all-to-all-start.1
  18.2 140.4 %all-gather.8.cloned.1.call-done = bf16[4096,2048]{1,0:T(8,128)(2,1)} async-done(((bf16[256,2048]{1,0:T(8,128)(2,1)}), bf16[4096,2048]{1,0:T(8,128)(2,1)}) %all-gather.8.cloned.1.call-update) | async-done | bytes 16777232 | tf_op jit(solution)/shard_map/all_gather | solution.py:46
  158.6 21.1 %copy.76 = bf16[2048,4096]{1,0:T(8,128)(2,1)} copy(bf16[2048,4096]{0,1:T(8,128)(2,1)} %bitcast.101) | data formatting | bytes 33554432 | tf_op jit(solution)/shard_map/dot_general | solution.py:53
  179.8 8.3 multiply_reduce_fusion.2
  189.4 1.5 multiply_convert_fusion
  190.9 2.1 reshape.100
  193.0 2.8 copy.77
  195.8 4.3 all-to-all-start.3
  200.2 98.0 %all-gather.6.cloned.1.call-done = bf16[4096,2048]{1,0:T(8,128)(2,1)} async-done(((bf16[256,2048]{1,0:T(8,128)(2,1)}), bf16[4096,2048]{1,0:T(8,128)(2,1)}) %all-gather.6.cloned.1.call-update) | async-done | bytes 16777232 | tf_op jit(solution)/shard_map/all_gather | solution.py:45
  298.2 21.0 %copy.72 = bf16[2048,4096]{1,0:T(8,128)(2,1)} copy(bf16[2048,4096]{0,1:T(8,128)(2,1)} %bitcast.102) | data formatting | bytes 33554432 | tf_op jit(solution)/shard_map/dot_general | solution.py:50
  319.1 8.3 multiply_reduce_fusion.3
  328.7 1.5 multiply_convert_fusion.1
  331.6 1.8 copy.73
  333.4 4.1 all-to-all-start.2
  337.4 101.2 %all-gather.4.cloned.1.call-done = bf16[4096,2048]{1,0:T(8,128)(2,1)} async-done(((bf16[256,2048]{1,0:T(8,128)(2,1)}), bf16[4096,2048]{1,0:T(8,128)(2,1)}) %all-gather.4.cloned.1.call-update) | async-done | bytes 16777232 | tf_op jit(solution)/shard_map/all_gather | solution.py:47
  438.6 8.3 fusion.15
  448.3 5.1 all-to-all-start
  453.4 2.2 copy.71
  455.7 2.2 copy.79
  458.8 2.0 fusion.28
  460.8 15.5 %all-to-all-done = bf16[2,128,16,128]{3,2,0,1:T(8,128)(2,1)} async-done(((bf16[2,128,16,128]{3,2,0,1:T(8,128)(2,1)}), bf16[2,128,16,128]{3,2,0,1:T(8,128)(2,1)}, u32[]{:S(2)}, u32[]{:S(2)}) %all-to-all-start) | async-done | bytes 1048608 | tf_op jit(solution)/shard_map/all_to_all | solution.py:68
  476.3 2.3 copy.68
  482.1 6.8 all-to-all-start.4
  488.9 3.0 fusion.17
  493.3 18.5 %all-to-all-done.4 = bf16[32,8,16,128]{3,2,1,0:T(8,128)(2,1)} async-done(((bf16[32,8,16,128]{3,2,1,0:T(8,128)(2,1)}), bf16[32,8,16,128]{3,2,1,0:T(8,128)(2,1)}, u32[]{:S(2)}, u32[]{:S(2)}) %all-to-all-start.4) | async-done | bytes 1048608 | tf_op jit(solution)/shard_map/all_to_all | solution.py:73
  511.8 6.8 all-to-all-start.5
  518.7 2.0 fusion.18
  525.0 2.9 copy.83
  527.9 13.7 %all-to-all-done.5 = bf16[32,8,16,128]{3,2,1,0:T(8,128)(2,1)} async-done(((bf16[32,8,16,128]{3,2,1,0:T(8,128)(2,1)}), bf16[32,8,16,128]{3,2,1,0:T(8,128)(2,1)}, u32[]{:S(2)}, u32[]{:S(2)}) %all-to-all-start.5) | async-done | bytes 1048608 | tf_op jit(solution)/shard_map/all_to_all | solution.py:74
  541.6 6.8 all-to-all-start.6
  551.4 2.9 copy.86
  554.3 2.8 multiply_reduce_fusion.1
  560.0 1.5 fusion.6
  561.6 1.5 fusion.7
  563.1 8.2 all-to-all-done.6
  572.9 2.3 copy.90
  575.1 2.2 copy.89
  577.4 21.3 %convert_bitcast_fusion = bf16[4096,6144]{0,1:T(8,128)(2,1)} fusion(bf16[256,4096]{1,0:T(8,128)(2,1)S(1)} %bitcast.98, bf16[256,2048]{1,0:T(8,128)(2,1)S(1)} %bitcast.107, bf16[256,2048]{1,0:T(8,128)(2,1)} %copy.90, bf16[256,2048]{1,0:T(8,128)(2,1)} %copy.89), kind=kOutput, calls=%fused_computation | convolution fusion | flops 12919504896 | bytes 55574528 | tf_op jit(solution)/shard_map/dot_general | solution.py:100
  598.8 8.6 reduce-scatter.3.cloned.1.call-start
  607.3 14.3 %fusion.29 = f32[256,4096]{1,0:T(8,128)} fusion(bf16[256,2048]{0,1:T(8,128)(2,1)S(1)} %bitcast.119, bf16[4096,2048]{1,0:T(8,128)(2,1)} %all-gather.6.cloned.1.call-done), kind=kOutput, calls=%fused_computation.48 | convolution fusion | flops 4294967296 | bytes 22020096 | tf_op jit(solution)/shard_map/dot_general | solution.py:85
  621.7 23.8 %convolution_add_fusion.1 = f32[256,4096]{1,0:T(8,128)} fusion(f32[256,4096]{1,0:T(8,128)} %fusion.29, bf16[256,2048]{0,1:T(8,128)(2,1)S(1)} %bitcast.121, bf16[4096,2048]{1,0:T(8,128)(2,1)} %all-gather.8.cloned.1.call-done), kind=kOutput, calls=%fused_computation.2 | convolution fusion | flops 4296015872 | bytes 26214400 | tf_op jit(solution)/shard_map/dot_general | solution.py:86
  645.5 23.4 %fusion = bf16[256,4096]{1,0:T(8,128)(2,1)} fusion(f32[256,4096]{1,0:T(8,128)} %convolution_add_fusion.1, bf16[4096,2048]{1,0:T(8,128)(2,1)} %all-gather.4.cloned.1.call-done, bf16[32,8,16,128]{3,2,1,0:T(8,128)(2,1)S(1)} %bitcast.115), kind=kOutput, calls=%fused_computation.3 | convolution fusion | flops 4297064448 | bytes 24117248 | tf_op jit(solution)/shard_map/dot_general | solution.py:89
  669.0 397.5 %reduce-scatter.5.cloned.1.call-done = bf16[256,6144]{0,1:T(8,128)(2,1)} async-done(((bf16[4096,6144]{0,1:T(8,128)(2,1)}), bf16[256,6144]{0,1:T(8,128)(2,1)}) %reduce-scatter.5.cloned.1.call-update) | async-done | bytes 3145744 | tf_op jit(solution)/shard_map/reduce_scatter | solution.py:101
  1066.4 4.4 fusion.27
  1070.8 2.9 copy.91
  1073.7 1.8 copy.92
  1075.5 3.0 copy.93
  1078.6 21.6 %reduce-scatter.3.cloned.1.call-done = bf16[2,128,2048]{2,1,0:T(8,128)(2,1)} async-done(((bf16[2,128,4096]{2,1,0:T(8,128)(2,1)}), bf16[2,128,2048]{2,1,0:T(8,128)(2,1)}) %reduce-scatter.3.cloned.1.call-update) | async-done | bytes 1048592 | tf_op jit(solution)/shard_map/reduce_scatter | solution.py:92
  (82 shorter events, 26.5 us)
Async XLA Ops:
  7.2 172.6 %copy-start = (bf16[2,128,4096]{2,1,0:T(8,128)(2,1)S(1)}, bf16[2,128,4096]{2,1,0:T(8,128)(2,1)}, u32[]{:S(2)}) copy-start(bf16[2,128,4096]{2,1,0:T(8,128)(2,1)} %param.7) | copy-start | bytes 6291460
  7.2 2.2 copy-start.20
  7.2 151.4 %all-gather.8.cloned.1.call-start = ((), (), s32[]{:S(2)}) async-start(), calls=%async_computation.11 | async-start | bytes 17825792 | tf_op jit(solution)/shard_map/all_gather | solution.py:46
  7.9 290.2 %all-gather.6.cloned.1.call-start = ((), (), s32[]{:S(2)}) async-start(), calls=%async_computation.10 | async-start | bytes 17825792 | tf_op jit(solution)/shard_map/all_gather | solution.py:45
  8.7 430.0 %all-gather.4.cloned.1.call-start = ((), (), s32[]{:S(2)}) async-start(), calls=%async_computation.9 | async-start | bytes 17825792 | tf_op jit(solution)/shard_map/all_gather | solution.py:47
  10.8 185.0 %all-to-all-start.1 = ((bf16[2,128,16,128]{3,2,0,1:T(8,128)(2,1)}), bf16[2,128,16,128]{3,2,0,1:T(8,128)(2,1)S(1)}, u32[]{:S(2)}, u32[]{:S(2)}) async-start(bf16[2,128,16,128]{3,2,0,1:T(8,128)(2,1)} %copy.95), calls=%async_computation.1 | async-start | bytes 2097152 | tf_op jit(solution)/shard_map/all_to_all | solution.py:69
  179.8 9.6 copy-start.22
  188.0 1.4 copy-start.2
  195.8 123.3 %copy-start.9 = (bf16[2,128,16,128]{3,2,0,1:T(8,128)(2,1)}, bf16[2,128,16,128]{3,2,0,1:T(8,128)(2,1)S(1)}, u32[]{:S(2)}) copy-start(bf16[2,128,16,128]{3,2,0,1:T(8,128)(2,1)S(1)} %all-to-all-done.1) | copy-start | bytes 3145732
  195.8 137.6 %all-to-all-start.3 = ((bf16[2,128,16,128]{3,2,0,1:T(8,128)(2,1)}), bf16[2,128,16,128]{3,2,0,1:T(8,128)(2,1)}, u32[]{:S(2)}, u32[]{:S(2)}) async-start(bf16[2,128,16,128]{3,2,0,1:T(8,128)(2,1)} %copy.77), calls=%async_computation.3 | async-start | bytes 2097152 | tf_op jit(solution)/shard_map/all_to_all | solution.py:67
  319.1 9.6 copy-start.21
  327.4 1.3 copy-start.4
  333.4 114.9 %all-to-all-start.2 = ((bf16[2,128,16,128]{3,2,0,1:T(8,128)(2,1)}), bf16[2,128,16,128]{3,2,0,1:T(8,128)(2,1)S(1)}, u32[]{:S(2)}, u32[]{:S(2)}) async-start(bf16[2,128,16,128]{3,2,0,1:T(8,128)(2,1)} %copy.73), calls=%async_computation.2 | async-start | bytes 2097152 | tf_op jit(solution)/shard_map/all_to_all | solution.py:66
  448.3 5.1 copy-start.10
  448.3 28.0 %all-to-all-start = ((bf16[2,128,16,128]{3,2,0,1:T(8,128)(2,1)}), bf16[2,128,16,128]{3,2,0,1:T(8,128)(2,1)}, u32[]{:S(2)}, u32[]{:S(2)}) async-start(bf16[2,128,16,128]{3,2,0,1:T(8,128)(2,1)} %copy.67), calls=%async_computation | async-start | bytes 2097152 | tf_op jit(solution)/shard_map/all_to_all | solution.py:68
  453.4 4.5 copy-start.11
  457.8 3.0 copy-start.17
  458.8 2.0 copy-start.16
  476.3 2.3 copy-start.8
  478.6 1.2 copy-start.18
  479.4 1.3 copy-start.19
  482.1 29.8 %all-to-all-start.4 = ((bf16[32,8,16,128]{3,2,1,0:T(8,128)(2,1)}), bf16[32,8,16,128]{3,2,1,0:T(8,128)(2,1)}, u32[]{:S(2)}, u32[]{:S(2)}) async-start(bf16[32,8,16,128]{3,2,1,0:T(8,128)(2,1)} %copy.81), calls=%async_computation.4 | async-start | bytes 2097152 | tf_op jit(solution)/shard_map/all_to_all | solution.py:73
  511.8 29.8 %all-to-all-start.5 = ((bf16[32,8,16,128]{3,2,1,0:T(8,128)(2,1)}), bf16[32,8,16,128]{3,2,1,0:T(8,128)(2,1)}, u32[]{:S(2)}, u32[]{:S(2)}) async-start(bf16[32,8,16,128]{3,2,1,0:T(8,128)(2,1)} %copy.84), calls=%async_computation.5 | async-start | bytes 2097152 | tf_op jit(solution)/shard_map/all_to_all | solution.py:74
  541.6 29.7 %all-to-all-start.6 = ((bf16[32,8,16,128]{3,2,1,0:T(8,128)(2,1)}), bf16[32,8,16,128]{3,2,1,0:T(8,128)(2,1)S(1)}, u32[]{:S(2)}, u32[]{:S(2)}) async-start(bf16[32,8,16,128]{3,2,1,0:T(8,128)(2,1)} %copy.87), calls=%async_computation.6 | async-start | bytes 2097152 | tf_op jit(solution)/shard_map/all_to_all | solution.py:75
  548.4 518.0 %reduce-scatter.5.cloned.1.call-start = ((), (), s32[]{:S(2)}) async-start(), calls=%async_computation.13 | async-start | bytes 53477376 | tf_op jit(solution)/shard_map/reduce_scatter | solution.py:101
  554.3 2.9 copy-start.3
  554.3 3.5 copy-start.7
  557.8 1.6 copy-start.5
  557.8 2.2 copy-start.6
  571.6 1.0 copy-start.12
  598.7 8.6 copy-start.14
  598.8 22.9 %copy-start.15 = (bf16[256,16,128]{0,2,1:T(8,128)(2,1)S(1)}, bf16[256,16,128]{0,2,1:T(8,128)(2,1)}, u32[]{:S(2)}) copy-start(bf16[256,16,128]{0,2,1:T(8,128)(2,1)} %fusion.7) | copy-start | bytes 3145732
  598.8 501.4 %reduce-scatter.3.cloned.1.call-start = ((), (), s32[]{:S(2)}) async-start(), calls=%async_computation.12 | async-start | bytes 3145728 | tf_op jit(solution)/shard_map/reduce_scatter | solution.py:92
  621.7 23.8 %copy-start.13 = (bf16[16,2,8,16,128]{4,3,2,0,1:T(8,128)(2,1)S(1)}, bf16[16,2,8,16,128]{4,3,2,0,1:T(8,128)(2,1)}, u32[]{:S(2)}) copy-start(bf16[16,2,8,16,128]{4,3,2,0,1:T(8,128)(2,1)} %copy-done.12) | copy-start | bytes 3145732
  1075.5 24.7 %copy-start.1 = (bf16[2,128,4096]{2,1,0:T(8,128)(2,1)S(1)}, bf16[2,128,4096]{2,1,0:T(8,128)(2,1)}, u32[]{:S(2)}) copy-start(bf16[2,128,4096]{2,1,0:T(8,128)(2,1)} %param.7) | copy-start | bytes 6291460
Sparse Core Ops, SparseCore 0:
  10.2 148.4 all-gather.7
  160.8 137.3 all-gather.5
  300.3 138.2 all-gather.3
  598.9 467.5 reduce-scatter.4
  1069.1 31.0 reduce-scatter.2
where the time goes:
time: 1120 us; the launch traced here: 1110 us
  waiting for transfers between devices  817 us (73%)
  matrix products  116 us (10%)
  local copies, waits for them, and re-layouts  97.5 us (9%)
  starting transfers between devices  50 us (4%)
  between operations  14.4 us (1%)
  other arithmetic  12.2 us (1%)
    reduce_scatter x1, waiting for transfers between devices, body(): lax.psum_scatter(term.astype(jnp.bfloat16), 'frame', scatter_dimension=0,...  397 us
    all_gather x1, waiting for transfers between devices, body(): lax.all_gather(w_key, 'frame', axis=0, tiled=True)  140 us
    all_gather x1, waiting for transfers between devices, body(): lax.all_gather(w_value, 'frame', axis=0, tiled=True)  101 us
    all_gather x1, waiting for transfers between devices, body(): lax.all_gather(w_query, 'frame', axis=0, tiled=True)  98 us
    dot_general x1, matrix products, body(): lax.dot_general(d_k_raw, full_key, contract, preferred_element_type=jnp.f...  23.8 us
    dot_general x1, matrix products, body(): lax.dot_general(d_v_rows, full_value, contract, preferred_element_type=jn...  23.4 us
  transfers between devices with their start and end apart: 12, of which 9 were waited for; matrix products, arithmetic and copies ran while one was open for 17% of the time, Pallas kernels for 0%

commit v1 on v0

v1 whole, which is shorter than its diff:
```python
import math

import jax
import jax.numpy as jnp
from jax import lax
from jax.sharding import Mesh, PartitionSpec as P

HD = 128


epsilon = 1e-06


def scaled(raw, gain):
    inverse = lax.rsqrt(jnp.mean(raw * raw, axis=-1, keepdims=True) + epsilon)
    return raw * inverse * gain


def attend(query, key_norm, value):
    factor = 1.0 / math.sqrt(query.shape[-1])
    scores = jnp.einsum("fphd,gphd->phfg", query, key_norm) * factor
    expon = jnp.exp(scores)
    weights = expon / jnp.sum(expon, axis=-1, keepdims=True)
    return jnp.einsum("phfg,gphd->fphd", weights, value)


def attend_back(query, key_norm, value, cotan):
    _, pull = jax.vjp(
        attend, query.astype(jnp.float32), key_norm.astype(jnp.float32), value.astype(jnp.float32)
    )
    grads = pull(cotan.astype(jnp.float32))
    return (
        grads[0].astype(jnp.bfloat16),
        grads[1].astype(jnp.bfloat16),
        grads[2].astype(jnp.bfloat16),
    )


def line_split(n_frame, heads_here):
    part = 1
    while (
        4 * part * part <= n_frame
        and n_frame % (2 * part) == 0
        and heads_here % (2 * part) == 0
    ):
        part *= 2
    return part


def make_body(n_a, n_b):
    def body(activations, w_query, w_key, w_value, q_gain, k_gain, grad_attn):
        frames_here, patches, width = activations.shape
        rows_here, head_cols = w_query.shape
        cols = head_cols // n_a
        heads = cols // HD
        frames = frames_here * n_a
        tokens = frames * patches

        def stacked(x):
            return jnp.concatenate([x[:, i * cols : (i + 1) * cols] for i in range(n_a)], axis=0)

        def exchange(x):
            return lax.all_to_all(x, "fa", split_axis=0, concat_axis=0, tiled=True)

        acts = lax.all_gather(activations.reshape(-1, width), "fa", axis=0, tiled=True)
        mine = [exchange(stacked(w)) for w in (w_query, w_key, w_value)]
        acts, mine = lax.optimization_barrier((acts, mine))
        wq, wk, wv = (lax.all_gather(m, "fb", axis=0, tiled=True) for m in mine)

        def blocks(x, order):
            return jnp.concatenate(
                [x[:, i * rows_here : (i + 1) * rows_here] for i in order], axis=1
            )

        rows = blocks(acts, [i * n_b + j for j in range(n_b) for i in range(n_a)])

        def spread(x):
            return lax.all_to_all(x, "fb", split_axis=1, concat_axis=0, tiled=True)

        def back(x):
            return lax.all_to_all(x, "fb", split_axis=0, concat_axis=1, tiled=True)

        shape4 = (frames, patches, heads, HD)
        cotan = exchange(stacked(grad_attn.reshape(-1, head_cols)))
        cotan = spread(cotan.reshape(shape4))

        q_raw = jnp.dot(rows, wq, preferred_element_type=jnp.float32).reshape(tokens, heads, HD)
        q_norm = spread(scaled(q_raw, q_gain).astype(jnp.bfloat16).reshape(shape4))
        k_raw = jnp.dot(rows, wk, preferred_element_type=jnp.float32).reshape(tokens, heads, HD)
        k_norm = spread(scaled(k_raw, k_gain).astype(jnp.bfloat16).reshape(shape4))
        value = jnp.dot(rows, wv, preferred_element_type=jnp.float32)
        value = spread(value.astype(jnp.bfloat16).reshape(shape4))

        grads = attend_back(q_norm, k_norm, value, cotan)
        d_val, d_qn, d_kn = back(grads[2]), back(grads[0]), back(grads[1])

        _, pull_query = jax.vjp(lambda raw: scaled(raw, q_gain), q_raw)
        _, pull_key = jax.vjp(lambda raw: scaled(raw, k_gain), k_raw)
        d_q = pull_query(d_qn.reshape(tokens, heads, HD).astype(jnp.float32))[0]
        d_q = d_q.astype(jnp.bfloat16).reshape(tokens, cols)
        d_k = pull_key(d_kn.reshape(tokens, heads, HD).astype(jnp.float32))[0]
        d_k = d_k.astype(jnp.bfloat16).reshape(tokens, cols)
        d_v = d_val.reshape(tokens, cols)

        def weight_grad(d):
            term = lax.dot_general(
                rows, d, (((0,), (0,)), ((), ())), preferred_element_type=jnp.float32
            ).astype(jnp.bfloat16)
            return lax.psum_scatter(term, "fb", scatter_dimension=0, tiled=True)

        def regroup(summed):
            out = exchange(summed)
            out = [out[i * rows_here : (i + 1) * rows_here] for i in range(n_a)]
            return jnp.concatenate(out, axis=1).astype(jnp.float32)

        sum_v, sum_q, sum_k = weight_grad(d_v), weight_grad(d_q), weight_grad(d_k)

        contract = (((1,), (1,)), ((), ()))
        partial = lax.dot_general(d_q, wq, contract, preferred_element_type=jnp.float32)
        partial = partial + lax.dot_general(d_k, wk, contract, preferred_element_type=jnp.float32)
        partial = partial + lax.dot_general(d_v, wv, contract, preferred_element_type=jnp.float32)
        partial = blocks(
            partial.astype(jnp.bfloat16), [j * n_a + i for i in range(n_a) for j in range(n_b)]
        )
        partial, sum_q, sum_k, sum_v = lax.optimization_barrier((partial, sum_q, sum_k, sum_v))
        partial = lax.psum_scatter(partial, "head", scatter_dimension=1, tiled=True)
        grad_input = lax.psum_scatter(partial, "fa", scatter_dimension=0, tiled=True)
        grad_input = grad_input.reshape(frames_here, patches, -1)
        return (grad_input, regroup(sum_q), regroup(sum_k), regroup(sum_v))

    return body


def solution(mesh):
    n_frame, n_head = mesh.shape["frame"], mesh.shape["head"]

    def run(activations, w_query, w_key, w_value, q_gain, k_gain, grad_attn):
        n_a = line_split(n_frame, w_query.shape[1] // (HD * n_head))
        n_b = n_frame // n_a
        split = Mesh(mesh.devices.reshape(n_a, n_b, n_head), ("fa", "fb", "head"))
        frame = ("fa", "fb")
        placed = (
            P(frame, None, None),
            P(frame, "head"),
            P(frame, "head"),
            P(frame, "head"),
            P(),
            P(),
            P(frame, None, "head"),
        )
        return jax.shard_map(
            make_body(n_a, n_b),
            mesh=split,
            in_specs=placed,
            out_specs=(
                P(frame, None, "head"),
                P(frame, "head"),
                P(frame, "head"),
                P(frame, "head"),
            ),
            check_vma=False,
        )(activations, w_query, w_key, w_value, q_gain, k_gain, grad_attn)

    return run
```

time: 1120 us -> 835 us (0.75)
  waiting for transfers between devices: 817 us -> 303 us
  blocking collectives: 0 us -> 218 us
  local copies, waits for them, and re-layouts: 97.5 us -> 121 us
    reduce_scatter x2 -> x5, waiting for transfers between devices: 419 us -> 98.3 us  [the longest x1 98.3 us: body(): partial = lax.psum_scatter(partial, 'head', scatter_dimension=1, tiled=True)]
    all_gather x3 -> x4, waiting for transfers between devices: 340 us -> 32.9 us  [the longest x1 32.8 us: body(): lax.all_gather(activations.reshape(-1, width), 'fa', axis=0, tiled=True)]
    all_to_all x0 -> x5, blocking collectives: none -> 218 us  [the longest x4 201 us: exchange(): return lax.all_to_all(x, 'fa', split_axis=0, concat_axis=0, tiled=True)]
    all_to_all x7 -> x9, waiting for transfers between devices: 55.9 us -> 170 us  [the longest x3 132 us: exchange(): return lax.all_to_all(x, 'fa', split_axis=0, concat_axis=0, tiled=True)]
    unnamed x52 -> x86, local copies, waits for them, and re-layouts: 15.2 us -> 69.1 us
    dot_general x2 -> x0, local copies, waits for them, and re-layouts: 42.1 us -> none  [the longest x1 21.1 us: body(): jnp.dot(tok_rows, full_key, preferred_element_type=jnp.float32)]
    dot_general x7 -> x9, matrix products: 108 us -> 94.1 us  [the longest x3 29.3 us: weight_grad(): lax.dot_general(rows, d, (((0,), (0,)), ((), ())), preferred_element_type...]
    all_to_all x7 -> x9, starting transfers between devices: 41.3 us -> 38.3 us  [the longest x4 16.4 us: spread(): return lax.all_to_all(x, 'fb', split_axis=1, concat_axis=0, tiled=True)]
  transfers between devices with their start and end apart: 12 -> 18, of which waited for: 9 -> 9; matrix products, arithmetic and copies ran while one was open for 17% -> 27% of each run, Pallas kernels for 0% -> 0%
where the time goes in v1:
time: 835 us; the launch traced here: 826 us
  waiting for transfers between devices  303 us (36%)
  blocking collectives  218 us (26%)
  local copies, waits for them, and re-layouts  121 us (14%)
  matrix products  108 us (13%)
  starting transfers between devices  39.1 us (5%)
  other arithmetic  21.4 us (3%)
  between operations  14.9 us (2%)
    all_to_all x4, blocking collectives, exchange(): return lax.all_to_all(x, 'fa', split_axis=0, concat_axis=0, tiled=True)  201 us
    all_to_all x3, waiting for transfers between devices, exchange(): return lax.all_to_all(x, 'fa', split_axis=0, concat_axis=0, tiled=True)  132 us
    reduce_scatter x1, waiting for transfers between devices, body(): partial = lax.psum_scatter(partial, 'head', scatter_dimension=1, tiled=True)  98.3 us
    unnamed x86, local copies, waits for them, and re-layouts  69.1 us
    all_gather x1, waiting for transfers between devices, body(): lax.all_gather(activations.reshape(-1, width), 'fa', axis=0, tiled=True)  32.8 us
    dot_general x3, matrix products, weight_grad(): lax.dot_general(rows, d, (((0,), (0,)), ((), ())), preferred_element_type...  29.3 us
    all_to_all x2, waiting for transfers between devices, back(): return lax.all_to_all(x, 'fb', split_axis=0, concat_axis=1, tiled=True)  24 us
    dot_general x1, matrix products, body(): lax.dot_general(d_v, wv, contract, preferred_element_type=jnp.float32)  19.3 us
  transfers between devices with their start and end apart: 18, of which 9 were waited for; matrix products, arithmetic and copies ran while one was open for 27% of the time, Pallas kernels for 0%

profile of v1, /device:TPU:0, one launch (start us, length us, event | category | flops | bytes accessed | tf_op | source)
XLA Modules:
  0.0 826.1 jit_solution(18355085753302775006)
XLA Ops:
  10.2 6.3 all-to-all-start.2
  17.7 52.1 %all-to-all-done.2 = bf16[4,256,512]{2,1,0:T(8,128)(2,1)S(1)} async-done(((bf16[4,256,512]{2,1,0:T(8,128)(2,1)}), bf16[4,256,512]{2,1,0:T(8,128)(2,1)S(1)}, u32[]{:S(2)}, u32[]{:S(2)}) %all-to-all-start.2) | async-done | bytes 1048608 | tf_op jit(solution)/shard_map/all_to_all | solution.py:63
  69.8 3.5 all-to-all-start.3
  74.8 53.1 %all-to-all-done.3 = bf16[4,256,512]{2,1,0:T(8,128)(2,1)S(1)} async-done(((bf16[4,256,512]{2,1,0:T(8,128)(2,1)}), bf16[4,256,512]{2,1,0:T(8,128)(2,1)S(1)}, u32[]{:S(2)}, u32[]{:S(2)}) %all-to-all-start.3) | async-done | bytes 1048608 | tf_op jit(solution)/shard_map/all_to_all | solution.py:63
  127.9 61.8 %all_to_all.177 = bf16[4,256,512]{2,1,0:T(8,128)(2,1)} all-to-all(bf16[4,256,512]{2,1,0:T(8,128)(2,1)S(1)} %bitcast.205), channel_id=1, replica_groups=mesh['fa'=4,'fb'=4,'head'=2] {'fa'}, dimensions={0} | all-to-all | bytes 2097152 | tf_op jit(solution)/shard_map/all_to_all | solution.py:63
  189.7 32.8 %all-gather.5.cloned.1.call-done = bf16[1024,4096]{1,0:T(8,128)(2,1)} async-done(((bf16[256,4096]{1,0:T(8,128)(2,1)}), bf16[1024,4096]{1,0:T(8,128)(2,1)}) %all-gather.5.cloned.1.call-update) | async-done | bytes 8388624 | tf_op jit(solution)/shard_map/all_gather | solution.py:65
  224.7 28.6 %all_to_all.178 = bf16[4,256,512]{2,1,0:T(8,128)(2,1)S(1)} all-to-all(bf16[4,256,512]{2,1,0:T(8,128)(2,1)S(1)} %bitcast.206), channel_id=1, replica_groups=mesh['fa'=4,'fb'=4,'head'=2] {'fa'}, dimensions={0} | all-to-all | bytes 2097152 | tf_op jit(solution)/shard_map/all_to_all | solution.py:63
  254.9 3.5 all-to-all-start.1
  268.0 2.1 slice_dynamic-update-slice_fusion.26
  289.3 8.3 %multiply_reduce_fusion.2 = (f32[1024,4]{0,1:T(4,128)S(1)}, f32[1024,512]{0,1:T(8,128)S(1)}) fusion(bf16[1024,4096]{1,0:T(8,128)(2,1)} %slice_dynamic-update-slice_fusion.16, bf16[4096,512]{1,0:T(8,128)(2,1)} %all-gather.9.cloned.1.call-done), kind=kOutput, calls=%fused_computation.30 | convolution fusion | flops 4296011776 | bytes 14696448 | tf_op jit(solution)/shard_map/dot_general | solution.py:87
  300.6 4.6 copy.78
  305.2 3.4 multiply_convert_fusion.1
  308.6 4.6 all-to-all-start.6
  313.2 8.3 %multiply_reduce_fusion.1 = (f32[1024,4]{0,1:T(4,128)S(1)}, f32[1024,512]{0,1:T(8,128)S(1)}) fusion(bf16[1024,4096]{1,0:T(8,128)(2,1)} %slice_dynamic-update-slice_fusion.16, bf16[4096,512]{1,0:T(8,128)(2,1)} %all-gather.11.cloned.1.call-done), kind=kOutput, calls=%fused_computation.28 | convolution fusion | flops 4296011776 | bytes 14696448 | tf_op jit(solution)/shard_map/dot_general | solution.py:89
  323.6 4.6 copy.82
  328.2 3.3 multiply_convert_fusion
  331.5 7.9 all-to-all-done.6
  339.3 3.5 all-to-all-start.7
  342.9 10.0 %convolution_convert_fusion.3 = bf16[1024,512]{1,0:T(8,128)(2,1)} fusion(bf16[1024,4096]{1,0:T(8,128)(2,1)} %slice_dynamic-update-slice_fusion.16, bf16[4096,512]{1,0:T(8,128)(2,1)} %all-gather.7.cloned.1.call-done), kind=kOutput, calls=%fused_computation.31 | convolution fusion | flops 4295491584 | bytes 13631488 | tf_op jit(solution)/shard_map/dot_general | solution.py:91
  352.9 2.1 reshape.162
  355.1 2.6 copy.75
  358.6 4.8 all-to-all-start.5
  367.8 4.0 fusion.44
  371.8 6.1 all-to-all-done.5
  377.9 3.1 multiply_reduce_fusion
  383.9 4.3 all-to-all-start.8
  388.4 2.9 copy.91
  391.3 11.4 %all-to-all-done.8 = bf16[32,32,4,128]{3,2,1,0:T(4,128)(2,1)} async-done(((bf16[32,32,4,128]{3,2,1,0:T(4,128)(2,1)}), bf16[32,32,4,128]{3,2,1,0:T(4,128)(2,1)}, u32[]{:S(2)}, u32[]{:S(2)}) %all-to-all-start.8) | async-done | bytes 1048608 | tf_op jit(solution)/shard_map/all_to_all | solution.py:81
  408.6 2.9 copy.89
  411.5 2.7 fusion
  415.1 9.8 %convolution_convert_fusion.2 = bf16[4096,512]{1,0:T(8,128)(2,1)} fusion(bf16[1024,4096]{1,0:T(8,128)(2,1)} %slice_dynamic-update-slice_fusion.16, bf16[1024,512]{0,1:T(8,128)(2,1)S(1)} %fusion), kind=kOutput, calls=%fused_computation.3 | convolution fusion | flops 4297064448 | bytes 13631488 | tf_op jit(solution)/shard_map/dot_general | solution.py:106
  425.0 2.4 fusion.13
  427.9 17.1 %all_to_all.179 = bf16[32,32,4,128]{3,2,1,0:T(4,128)(2,1)S(1)} all-to-all(bf16[32,32,4,128]{3,2,1,0:T(4,128)(2,1)S(1)} %copy.98), channel_id=1, replica_groups=mesh['fa'=4,'fb'=4,'head'=2] {'fb'}, dimensions={0} | all-to-all | bytes 2097152 | tf_op jit(solution)/shard_map/all_to_all | solution.py:81
  445.4 9.8 %convolution_convert_fusion = bf16[4096,512]{1,0:T(8,128)(2,1)} fusion(bf16[1024,4096]{1,0:T(8,128)(2,1)} %slice_dynamic-update-slice_fusion.16, bf16[128,8,4,128]{3,2,1,0:T(4,128)(2,1)S(1)} %bitcast.196), kind=kOutput, calls=%fused_computation.1 | convolution fusion | flops 4297064448 | bytes 13631488 | tf_op jit(solution)/shard_map/dot_general | solution.py:106
  455.2 3.6 fusion.12
  460.3 4.3 all-to-all-start.9
  466.5 12.6 %all-to-all-done.9 = bf16[32,32,4,128]{3,2,1,0:T(4,128)(2,1)} async-done(((bf16[32,32,4,128]{3,2,1,0:T(4,128)(2,1)}), bf16[32,32,4,128]{3,2,1,0:T(4,128)(2,1)}, u32[]{:S(2)}, u32[]{:S(2)}) %all-to-all-start.9) | async-done | bytes 1048608 | tf_op jit(solution)/shard_map/all_to_all | solution.py:81
  485.9 2.9 copy.95
  488.7 3.4 fusion.3
  493.7 9.7 %convolution_convert_fusion.1 = bf16[4096,512]{1,0:T(8,128)(2,1)} fusion(bf16[1024,4096]{1,0:T(8,128)(2,1)} %slice_dynamic-update-slice_fusion.16, bf16[1024,512]{0,1:T(8,128)(2,1)S(1)} %fusion.1), kind=kOutput, calls=%fused_computation.2 | convolution fusion | flops 4297064448 | bytes 13631488 | tf_op jit(solution)/shard_map/dot_general | solution.py:106
  504.7 10.6 %fusion.46 = f32[1024,4096]{1,0:T(8,128)} fusion(bf16[1024,512]{0,1:T(8,128)(2,1)S(1)} %copy-done.16, bf16[4096,512]{1,0:T(8,128)(2,1)} %all-gather.11.cloned.1.call-done), kind=kOutput, calls=%fused_computation.128 | convolution fusion | flops 4294967296 | bytes 22020096 | tf_op jit(solution)/shard_map/dot_general | solution.py:120
  515.3 8.2 fusion.45
  523.5 19.3 %add_convert_fusion = bf16[1024,4096]{1,0:T(8,128)(2,1)} fusion(f32[1024,4096]{1,0:T(8,128)} %fusion.45, f32[1024,4096]{1,0:T(8,128)} %fusion.46, bf16[4096,512]{1,0:T(8,128)(2,1)} %all-gather.7.cloned.1.call-done, bf16[128,8,4,128]{3,2,1,0:T(4,128)(2,1)S(1)} %bitcast.197), kind=kOutput, calls=%fused_computation | convolution fusion | flops 4307550208 | bytes 47185920 | tf_op jit(solution)/shard_map/dot_general | solution.py:121
  573.7 98.3 %reduce-scatter.12.cloned.1.call-done = bf16[1024,2048]{1,0:T(8,128)(2,1)} async-done(((bf16[1024,4096]{1,0:T(8,128)(2,1)}), bf16[1024,2048]{1,0:T(8,128)(2,1)}) %reduce-scatter.12.cloned.1.call-update) | async-done | bytes 4194320 | tf_op jit(solution)/shard_map/reduce_scatter | solution.py:126
  672.0 57.3 %all_to_all.180 = bf16[4,256,512]{2,1,0:T(8,128)(2,1)S(1)} all-to-all(bf16[4,256,512]{2,1,0:T(8,128)(2,1)S(1)} %bitcast.215), channel_id=1, replica_groups=mesh['fa'=4,'fb'=4,'head'=2] {'fa'}, dimensions={0} | all-to-all | bytes 2097152 | tf_op jit(solution)/shard_map/all_to_all | solution.py:63
  729.4 53.5 %all_to_all.181 = bf16[4,256,512]{2,1,0:T(8,128)(2,1)S(1)} all-to-all(bf16[4,256,512]{2,1,0:T(8,128)(2,1)} %bitcast.216), channel_id=1, replica_groups=mesh['fa'=4,'fb'=4,'head'=2] {'fa'}, dimensions={0} | all-to-all | bytes 2097152 | tf_op jit(solution)/shard_map/all_to_all | solution.py:63
  782.8 3.5 all-to-all-start.13
  787.4 27.0 %all-to-all-done.13 = bf16[4,256,512]{2,1,0:T(8,128)(2,1)S(1)} async-done(((bf16[4,256,512]{2,1,0:T(8,128)(2,1)}), bf16[4,256,512]{2,1,0:T(8,128)(2,1)S(1)}, u32[]{:S(2)}, u32[]{:S(2)}) %all-to-all-start.13) | async-done | bytes 1048608 | tf_op jit(solution)/shard_map/all_to_all | solution.py:63
  (159 shorter events, 108.9 us)
Async XLA Ops:
  7.2 215.4 %all-gather.5.cloned.1.call-start = ((), (), s32[]{:S(2)}) async-start(), calls=%async_computation.19 | async-start | bytes 10485760 | tf_op jit(solution)/shard_map/all_gather | solution.py:65
  7.2 9.3 %copy-start.17 = (bf16[256,2048]{1,0:T(8,128)(2,1)S(1)}, bf16[256,2048]{1,0:T(8,128)(2,1)}, u32[]{:S(2)}) copy-start(bf16[256,2048]{1,0:T(8,128)(2,1)} %param.9) | copy-start | bytes 3145732
  10.2 59.6 %all-to-all-start.2 = ((bf16[4,256,512]{2,1,0:T(8,128)(2,1)}), bf16[4,256,512]{2,1,0:T(8,128)(2,1)S(1)}, u32[]{:S(2)}, u32[]{:S(2)}) async-start(bf16[4,256,512]{2,1,0:T(8,128)(2,1)} %bitcast.7), calls=%async_computation.2 | async-start | bytes 2097152 | tf_op jit(solution)/shard_map/all_to_all | solution.py:63
  69.8 119.9 %copy-start.5 = (bf16[4,256,512]{2,1,0:T(8,128)(2,1)}, bf16[4,256,512]{2,1,0:T(8,128)(2,1)S(1)}, u32[]{:S(2)}) copy-start(bf16[4,256,512]{2,1,0:T(8,128)(2,1)S(1)} %all-to-all-done.2) | copy-start | bytes 3145732
  69.8 58.1 %all-to-all-start.3 = ((bf16[4,256,512]{2,1,0:T(8,128)(2,1)}), bf16[4,256,512]{2,1,0:T(8,128)(2,1)S(1)}, u32[]{:S(2)}, u32[]{:S(2)}) async-start(bf16[4,256,512]{2,1,0:T(8,128)(2,1)} %bitcast.9), calls=%async_computation.3 | async-start | bytes 2097152 | tf_op jit(solution)/shard_map/all_to_all | solution.py:63
  73.4 215.9 %all-gather.9.cloned.1.call-start = ((), (), s32[]{:S(2)}) async-start(), calls=%async_computation.21 | async-start | bytes 5242880 | tf_op jit(solution)/shard_map/all_gather | solution.py:68
  127.9 94.7 %copy-start.4 = (bf16[4,256,512]{2,1,0:T(8,128)(2,1)}, bf16[4,256,512]{2,1,0:T(8,128)(2,1)S(1)}, u32[]{:S(2)}) copy-start(bf16[4,256,512]{2,1,0:T(8,128)(2,1)S(1)} %all-to-all-done.3) | copy-start | bytes 3145732
  222.6 90.6 %all-gather.11.cloned.1.call-start = ((), (), s32[]{:S(2)}) async-start(), calls=%async_computation.22 | async-start | bytes 5242880 | tf_op jit(solution)/shard_map/all_gather | solution.py:68
  254.9 53.8 %all-to-all-start.1 = ((bf16[8,128,4,128]{3,2,0,1:T(4,128)(2,1)}), bf16[8,128,4,128]{3,2,0,1:T(4,128)(2,1)S(1)}, u32[]{:S(2)}, u32[]{:S(2)}) async-start(bf16[8,128,4,128]{3,2,0,1:T(4,128)(2,1)} %copy.72), calls=%async_computation.1 | async-start | bytes 2097152 | tf_op jit(solution)/shard_map/all_to_all | solution.py:78
  258.4 84.5 %all-gather.7.cloned.1.call-start = ((), (), s32[]{:S(2)}) async-start(), calls=%async_computation.20 | async-start | bytes 5242880 | tf_op jit(solution)/shard_map/all_gather | solution.py:68
  297.6 7.6 copy-start
  298.9 6.4 copy-start.22
  308.6 12.9 %copy-start.6 = (bf16[8,128,4,128]{3,2,0,1:T(4,128)(2,1)}, bf16[8,128,4,128]{3,2,0,1:T(4,128)(2,1)S(1)}, u32[]{:S(2)}) copy-start(bf16[8,128,4,128]{3,2,0,1:T(4,128)(2,1)S(1)} %all-to-all-done.1) | copy-start | bytes 3145732
  308.6 30.7 %all-to-all-start.6 = ((bf16[8,128,4,128]{3,2,0,1:T(4,128)(2,1)}), bf16[8,128,4,128]{3,2,0,1:T(4,128)(2,1)}, u32[]{:S(2)}, u32[]{:S(2)}) async-start(bf16[8,128,4,128]{3,2,0,1:T(4,128)(2,1)} %multiply_convert_fusion.1), calls=%async_computation.6 | async-start | bytes 2097152 | tf_op jit(solution)/shard_map/all_to_all | solution.py:78
  321.9 6.4 copy-start.23
  339.3 18.3 %all-to-all-start.7 = ((bf16[8,128,4,128]{3,2,0,1:T(4,128)(2,1)}), bf16[8,128,4,128]{3,2,0,1:T(4,128)(2,1)S(1)}, u32[]{:S(2)}, u32[]{:S(2)}) async-start(bf16[8,128,4,128]{3,2,0,1:T(4,128)(2,1)} %multiply_convert_fusion), calls=%async_computation.7 | async-start | bytes 2097152 | tf_op jit(solution)/shard_map/all_to_all | solution.py:78
  357.6 1.0 copy-start.7
  358.6 19.3 %all-to-all-start.5 = ((bf16[8,128,4,128]{3,2,0,1:T(4,128)(2,1)}), bf16[8,128,4,128]{3,2,0,1:T(4,128)(2,1)}, u32[]{:S(2)}, u32[]{:S(2)}) async-start(bf16[8,128,4,128]{3,2,0,1:T(4,128)(2,1)} %copy.75), calls=%async_computation.5 | async-start | bytes 2097152 | tf_op jit(solution)/shard_map/all_to_all | solution.py:78
  363.4 3.4 copy-start.8
  366.8 1.0 copy-start.9
  367.2 4.5 copy-start.10
  377.9 3.2 copy-start.1
  377.9 3.2 copy-start.11
  381.0 1.3 copy-start.12
  383.9 18.8 %all-to-all-start.8 = ((bf16[32,32,4,128]{3,2,1,0:T(4,128)(2,1)}), bf16[32,32,4,128]{3,2,1,0:T(4,128)(2,1)}, u32[]{:S(2)}, u32[]{:S(2)}) async-start(bf16[32,32,4,128]{3,2,1,0:T(4,128)(2,1)} %copy.86), calls=%async_computation.8 | async-start | bytes 2097152 | tf_op jit(solution)/shard_map/all_to_all | solution.py:81
  388.1 185.5 %reduce-scatter.6.cloned.1.call-start = ((), (), s32[]{:S(2)}) async-start(), calls=%async_computation.23 | async-start | bytes 5242880 | tf_op jit(solution)/shard_map/reduce_scatter | solution.py:109
  404.4 2.1 copy-start.3
  414.1 1.0 copy-start.13
  424.9 148.7 %reduce-scatter.10.cloned.1.call-start = ((), (), s32[]{:S(2)}) async-start(), calls=%async_computation.25 | async-start | bytes 5242880 | tf_op jit(solution)/shard_map/reduce_scatter | solution.py:109
  460.3 18.8 %all-to-all-start.9 = ((bf16[32,32,4,128]{3,2,1,0:T(4,128)(2,1)}), bf16[32,32,4,128]{3,2,1,0:T(4,128)(2,1)}, u32[]{:S(2)}, u32[]{:S(2)}) async-start(bf16[32,32,4,128]{3,2,1,0:T(4,128)(2,1)} %copy.92), calls=%async_computation.9 | async-start | bytes 2097152 | tf_op jit(solution)/shard_map/all_to_all | solution.py:81
  464.6 109.0 %reduce-scatter.8.cloned.1.call-start = ((), (), s32[]{:S(2)}) async-start(), calls=%async_computation.24 | async-start | bytes 5242880 | tf_op jit(solution)/shard_map/reduce_scatter | solution.py:109
  488.7 3.5 copy-start.2
  492.7 1.0 copy-start.15
  503.4 1.2 copy-start.16
  503.5 11.8 %copy-start.14 = (bf16[1024,512]{0,1:T(8,128)(2,1)S(1)}, bf16[1024,512]{0,1:T(8,128)(2,1)}, u32[]{:S(2)}) copy-start(bf16[1024,512]{0,1:T(8,128)(2,1)} %copy-done.13) | copy-start | bytes 3145732
  503.5 168.5 %reduce-scatter.12.cloned.1.call-start = ((), (), s32[]{:S(2)}) async-start(), calls=%async_computation.26 | async-start | bytes 12582912 | tf_op jit(solution)/shard_map/reduce_scatter | solution.py:126
  504.7 10.6 %copy-start.24 = (bf16[4096,512]{1,0:T(8,128)(2,1)S(1)}, bf16[4096,512]{1,0:T(8,128)(2,1)}, u32[]{:S(2)}) copy-start(bf16[4096,512]{1,0:T(8,128)(2,1)} %all-gather.9.cloned.1.call-done) | copy-start | bytes 12582916
  573.7 98.4 %copy-start.18 = (bf16[1024,512]{1,0:T(8,128)(2,1)S(1)}, bf16[1024,512]{1,0:T(8,128)(2,1)}, u32[]{:S(2)}) copy-start(bf16[1024,512]{1,0:T(8,128)(2,1)} %reduce-scatter.6.cloned.1.call-done) | copy-start | bytes 3145732
  573.7 245.5 %reduce-scatter.14.cloned.1.call-start = ((), (), s32[]{:S(2)}) async-start(), calls=%async_computation.27 | async-start | bytes 5242880 | tf_op jit(solution)/shard_map/reduce_scatter | solution.py:127
  782.8 31.5 %all-to-all-start.13 = ((bf16[4,256,512]{2,1,0:T(8,128)(2,1)}), bf16[4,256,512]{2,1,0:T(8,128)(2,1)S(1)}, u32[]{:S(2)}, u32[]{:S(2)}) async-start(bf16[4,256,512]{2,1,0:T(8,128)(2,1)} %bitcast.214), calls=%async_computation.18 | async-start | bytes 2097152 | tf_op jit(solution)/shard_map/all_to_all | solution.py:63
  787.3 30.2 %copy-start.19 = (bf16[256,512]{1,0:T(8,128)(2,1)S(1)}, bf16[256,512]{1,0:T(8,128)(2,1)}, u32[]{:S(2)}) copy-start(bf16[256,512]{1,0:T(8,128)(2,1)} %get-tuple-element.29) | copy-start | bytes 786436
  787.3 30.2 %copy-start.20 = (bf16[256,512]{1,0:T(8,128)(2,1)S(1)}, bf16[256,512]{1,0:T(8,128)(2,1)}, u32[]{:S(2)}) copy-start(bf16[256,512]{1,0:T(8,128)(2,1)} %get-tuple-element.30) | copy-start | bytes 786436
  787.4 30.2 %copy-start.21 = (bf16[256,512]{1,0:T(8,128)(2,1)S(1)}, bf16[256,512]{1,0:T(8,128)(2,1)}, u32[]{:S(2)}) copy-start(bf16[256,512]{1,0:T(8,128)(2,1)} %get-tuple-element.31) | copy-start | bytes 786436
Sparse Core Ops, SparseCore 0:
  9.5 212.9 all-gather.4
  224.7 33.5 all-gather.8
  259.9 36.9 all-gather.10
  298.3 43.8 all-gather.6
  425.0 43.8 reduce-scatter.5
  471.4 45.2 reduce-scatter.9
  519.2 44.5 reduce-scatter.7
  573.8 98.1 reduce-scatter.11
  674.9 111.1 reduce-scatter.13

commit v2 on v1

--- a/solution.py
+++ b/solution.py
@@ -63,8 +63,11 @@
             return lax.all_to_all(x, "fa", split_axis=0, concat_axis=0, tiled=True)
 
         acts = lax.all_gather(activations.reshape(-1, width), "fa", axis=0, tiled=True)
-        mine = [exchange(stacked(w)) for w in (w_query, w_key, w_value)]
-        acts, mine = lax.optimization_barrier((acts, mine))
+        cotan = exchange(stacked(grad_attn.reshape(-1, head_cols)))
+        acts, cotan, *mine = lax.optimization_barrier(
+            (acts, cotan, exchange(stacked(w_query)), stacked(w_key), stacked(w_value))
+        )
+        mine[1:] = [exchange(m) for m in mine[1:]]
         wq, wk, wv = (lax.all_gather(m, "fb", axis=0, tiled=True) for m in mine)
 
         def blocks(x, order):
@@ -81,7 +84,6 @@
             return lax.all_to_all(x, "fb", split_axis=0, concat_axis=1, tiled=True)
 
         shape4 = (frames, patches, heads, HD)
-        cotan = exchange(stacked(grad_attn.reshape(-1, head_cols)))
         cotan = spread(cotan.reshape(shape4))
 
         q_raw = jnp.dot(rows, wq, preferred_element_type=jnp.float32).reshape(tokens, heads, HD)
@@ -124,9 +126,11 @@
         )
         partial, sum_q, sum_k, sum_v = lax.optimization_barrier((partial, sum_q, sum_k, sum_v))
         partial = lax.psum_scatter(partial, "head", scatter_dimension=1, tiled=True)
+        sums = (regroup(sum_q), regroup(sum_k), regroup(sum_v))
+        partial, sums = lax.optimization_barrier((partial, sums))
         grad_input = lax.psum_scatter(partial, "fa", scatter_dimension=0, tiled=True)
         grad_input = grad_input.reshape(frames_here, patches, -1)
-        return (grad_input, regroup(sum_q), regroup(sum_k), regroup(sum_v))
+        return (grad_input, *sums)
 
     return body
 

time: 835 us -> 754 us (0.903)
  blocking collectives: 218 us -> 107 us
  waiting for transfers between devices: 303 us -> 327 us
    all_to_all x4 -> x3, blocking collectives: 201 us -> 89.5 us  [exchange(): return lax.all_to_all(x, 'fa', split_axis=0, concat_axis=0, tiled=True)]
    reduce_scatter x1, waiting for transfers between devices: 98.3 us -> 6.34 us  [body(): partial = lax.psum_scatter(partial, 'head', scatter_dimension=1, tiled=True)]
    reduce_scatter x1, waiting for transfers between devices: 0.01 us -> 79.7 us  [body(): lax.psum_scatter(partial, 'fa', scatter_dimension=0, tiled=True)]
    all_gather x1, waiting for transfers between devices: 32.8 us -> 72.2 us  [body(): lax.all_gather(activations.reshape(-1, width), 'fa', axis=0, tiled=True)]
    all_to_all x3 -> x4, starting transfers between devices: 13.4 us -> 17 us  [exchange(): return lax.all_to_all(x, 'fa', split_axis=0, concat_axis=0, tiled=True)]
    all_to_all x3 -> x4, waiting for transfers between devices: 132 us -> 134 us  [exchange(): return lax.all_to_all(x, 'fa', split_axis=0, concat_axis=0, tiled=True)]
    unnamed x86 -> x82, local copies, waits for them, and re-layouts: 69.1 us -> 68.5 us
  transfers between devices with their start and end apart: 18 -> 19, of which waited for: 9 -> 11; matrix products, arithmetic and copies ran while one was open for 27% -> 30% of each run, Pallas kernels for 0% -> 0%
where the time goes in v2:
time: 754 us; the launch traced here: 744 us
  waiting for transfers between devices  327 us (43%)
  local copies, waits for them, and re-layouts  123 us (16%)
  blocking collectives  107 us (14%)
  matrix products  107 us (14%)
  starting transfers between devices  43.5 us (6%)
  other arithmetic  21.2 us (3%)
  between operations  14.9 us (2%)
    all_to_all x4, waiting for transfers between devices, exchange(): return lax.all_to_all(x, 'fa', split_axis=0, concat_axis=0, tiled=True)  134 us
    all_to_all x3, blocking collectives, exchange(): return lax.all_to_all(x, 'fa', split_axis=0, concat_axis=0, tiled=True)  89.5 us
    reduce_scatter x1, waiting for transfers between devices, body(): lax.psum_scatter(partial, 'fa', scatter_dimension=0, tiled=True)  79.7 us
    all_gather x1, waiting for transfers between devices, body(): lax.all_gather(activations.reshape(-1, width), 'fa', axis=0, tiled=True)  72.2 us
    unnamed x82, local copies, waits for them, and re-layouts  68.5 us
    dot_general x3, matrix products, weight_grad(): lax.dot_general(rows, d, (((0,), (0,)), ((), ())), preferred_element_type...  29.3 us
    all_to_all x2, waiting for transfers between devices, back(): return lax.all_to_all(x, 'fb', split_axis=0, concat_axis=1, tiled=True)  24.8 us
    dot_general x1, matrix products, body(): lax.dot_general(d_v, wv, contract, preferred_element_type=jnp.float32)  19.3 us
  transfers between devices with their start and end apart: 19, of which 11 were waited for; matrix products, arithmetic and copies ran while one was open for 30% of the time, Pallas kernels for 0%

profile of v2, /device:TPU:0, one launch (start us, length us, event | category | flops | bytes accessed | tf_op | source)
XLA Modules:
  0.0 743.8 jit_solution(7648525101042112511)
XLA Ops:
  10.7 6.5 all-to-all-start
  18.3 52.4 %all-to-all-done = bf16[4,256,512]{1,2,0:T(8,128)(2,1)S(1)} async-done(((bf16[4,256,512]{1,2,0:T(8,128)(2,1)}), bf16[4,256,512]{1,2,0:T(8,128)(2,1)S(1)}, u32[]{:S(2)}, u32[]{:S(2)}) %all-to-all-start) | async-done | bytes 1048608 | tf_op jit(solution)/shard_map/all_to_all | solution.py:63
  70.7 3.5 all-to-all-start.1
  77.6 50.9 %all-to-all-done.1 = bf16[4,256,512]{2,1,0:T(8,128)(2,1)S(1)} async-done(((bf16[4,256,512]{2,1,0:T(8,128)(2,1)}), bf16[4,256,512]{2,1,0:T(8,128)(2,1)S(1)}, u32[]{:S(2)}, u32[]{:S(2)}) %all-to-all-start.1) | async-done | bytes 1048608 | tf_op jit(solution)/shard_map/all_to_all | solution.py:63
  128.6 72.2 %all-gather.5.cloned.1.call-done = bf16[1024,4096]{1,0:T(8,128)(2,1)} async-done(((bf16[256,4096]{1,0:T(8,128)(2,1)}), bf16[1024,4096]{1,0:T(8,128)(2,1)}) %all-gather.5.cloned.1.call-update) | async-done | bytes 8388624 | tf_op jit(solution)/shard_map/all_gather | solution.py:65
  200.8 30.5 %all_to_all.180 = bf16[4,256,512]{2,1,0:T(8,128)(2,1)} all-to-all(bf16[4,256,512]{2,1,0:T(8,128)(2,1)} %bitcast.212), channel_id=1, replica_groups=mesh['fa'=4,'fb'=4,'head'=2] {'fa'}, dimensions={0} | all-to-all | bytes 2097152 | tf_op jit(solution)/shard_map/all_to_all | solution.py:63
  231.4 3.5 all-to-all-start.3
  239.1 2.2 copy.107
  252.9 7.3 all-to-all-done.3
  260.2 3.5 all-to-all-start.2
  279.6 8.3 %multiply_reduce_fusion.2 = (f32[1024,4]{0,1:T(4,128)S(1)}, f32[1024,512]{0,1:T(8,128)S(1)}) fusion(bf16[1024,4096]{1,0:T(8,128)(2,1)} %slice_dynamic-update-slice_fusion.16, bf16[4096,512]{1,0:T(8,128)(2,1)} %all-gather.9.cloned.1.call-done), kind=kOutput, calls=%fused_computation.30 | convolution fusion | flops 4296011776 | bytes 14696448 | tf_op jit(solution)/shard_map/dot_general | solution.py:89
  290.9 4.6 copy.113
  295.5 3.3 multiply_convert_fusion.1
  298.8 4.5 all-to-all-start.5
  303.4 8.3 %multiply_reduce_fusion.1 = (f32[1024,4]{0,1:T(4,128)S(1)}, f32[1024,512]{0,1:T(8,128)S(1)}) fusion(bf16[1024,4096]{1,0:T(8,128)(2,1)} %slice_dynamic-update-slice_fusion.16, bf16[4096,512]{1,0:T(8,128)(2,1)} %all-gather.11.cloned.1.call-done), kind=kOutput, calls=%fused_computation.28 | convolution fusion | flops 4296011776 | bytes 14696448 | tf_op jit(solution)/shard_map/dot_general | solution.py:91
  314.6 4.6 copy.117
  319.2 3.3 multiply_convert_fusion
  324.4 4.3 all-to-all-start.7
  328.7 10.0 %convolution_convert_fusion.3 = bf16[1024,512]{1,0:T(8,128)(2,1)} fusion(bf16[1024,4096]{1,0:T(8,128)(2,1)} %slice_dynamic-update-slice_fusion.16, bf16[4096,512]{1,0:T(8,128)(2,1)} %all-gather.7.cloned.1.call-done), kind=kOutput, calls=%fused_computation.31 | convolution fusion | flops 4295491584 | bytes 13631488 | tf_op jit(solution)/shard_map/dot_general | solution.py:93
  338.7 2.1 reshape.161
  340.9 2.6 copy.110
  343.4 4.8 all-to-all-start.4
  351.9 4.0 fusion.44
  355.9 6.8 all-to-all-done.4
  362.7 2.8 multiply_reduce_fusion
  368.3 4.3 all-to-all-start.8
  372.8 2.9 copy.126
  375.7 11.4 %all-to-all-done.8 = bf16[32,32,4,128]{3,2,1,0:T(4,128)(2,1)} async-done(((bf16[32,32,4,128]{3,2,1,0:T(4,128)(2,1)}), bf16[32,32,4,128]{3,2,1,0:T(4,128)(2,1)}, u32[]{:S(2)}, u32[]{:S(2)}) %all-to-all-start.8) | async-done | bytes 1048608 | tf_op jit(solution)/shard_map/all_to_all | solution.py:84
  393.0 2.9 copy.124
  395.9 2.7 fusion
  399.5 9.8 %convolution_convert_fusion.2 = bf16[4096,512]{1,0:T(8,128)(2,1)} fusion(bf16[1024,4096]{1,0:T(8,128)(2,1)} %slice_dynamic-update-slice_fusion.16, bf16[1024,512]{0,1:T(8,128)(2,1)S(1)} %fusion), kind=kOutput, calls=%fused_computation.3 | convolution fusion | flops 4297064448 | bytes 13631488 | tf_op jit(solution)/shard_map/dot_general | solution.py:108
  412.0 17.1 %all_to_all.181 = bf16[32,32,4,128]{3,2,1,0:T(4,128)(2,1)S(1)} all-to-all(bf16[32,32,4,128]{3,2,1,0:T(4,128)(2,1)S(1)} %copy.133), channel_id=1, replica_groups=mesh['fa'=4,'fb'=4,'head'=2] {'fb'}, dimensions={0} | all-to-all | bytes 2097152 | tf_op jit(solution)/shard_map/all_to_all | solution.py:84
  429.5 9.8 %convolution_convert_fusion = bf16[4096,512]{1,0:T(8,128)(2,1)} fusion(bf16[1024,4096]{1,0:T(8,128)(2,1)} %slice_dynamic-update-slice_fusion.16, bf16[128,8,4,128]{3,2,1,0:T(4,128)(2,1)S(1)} %bitcast.197), kind=kOutput, calls=%fused_computation.1 | convolution fusion | flops 4297064448 | bytes 13631488 | tf_op jit(solution)/shard_map/dot_general | solution.py:108
  439.3 3.6 fusion.12
  444.4 4.3 all-to-all-start.9
  450.5 13.4 %all-to-all-done.9 = bf16[32,32,4,128]{3,2,1,0:T(4,128)(2,1)} async-done(((bf16[32,32,4,128]{3,2,1,0:T(4,128)(2,1)}), bf16[32,32,4,128]{3,2,1,0:T(4,128)(2,1)}, u32[]{:S(2)}, u32[]{:S(2)}) %all-to-all-start.9) | async-done | bytes 1048608 | tf_op jit(solution)/shard_map/all_to_all | solution.py:84
  470.4 2.9 copy.130
  473.3 3.0 fusion.3
  477.8 9.7 %convolution_convert_fusion.1 = bf16[4096,512]{1,0:T(8,128)(2,1)} fusion(bf16[1024,4096]{1,0:T(8,128)(2,1)} %slice_dynamic-update-slice_fusion.16, bf16[1024,512]{0,1:T(8,128)(2,1)S(1)} %fusion.1), kind=kOutput, calls=%fused_computation.2 | convolution fusion | flops 4297064448 | bytes 13631488 | tf_op jit(solution)/shard_map/dot_general | solution.py:108
  488.7 10.6 %fusion.46 = f32[1024,4096]{1,0:T(8,128)} fusion(bf16[1024,512]{0,1:T(8,128)(2,1)S(1)} %copy-done.13, bf16[4096,512]{1,0:T(8,128)(2,1)} %all-gather.11.cloned.1.call-done), kind=kOutput, calls=%fused_computation.128 | convolution fusion | flops 4294967296 | bytes 22020096 | tf_op jit(solution)/shard_map/dot_general | solution.py:122
  499.3 8.1 %fusion.45 = f32[1024,4096]{1,0:T(8,128)} fusion(bf16[1024,512]{0,1:T(8,128)(2,1)S(1)} %copy-done.11, bf16[4096,512]{1,0:T(8,128)(2,1)S(1)} %copy-done.22), kind=kOutput, calls=%fused_computation.127 | convolution fusion | flops 4294967296 | bytes 22020096 | tf_op jit(solution)/shard_map/dot_general | solution.py:121
  507.4 19.3 %add_convert_fusion = bf16[1024,4096]{1,0:T(8,128)(2,1)} fusion(f32[1024,4096]{1,0:T(8,128)} %fusion.45, f32[1024,4096]{1,0:T(8,128)} %fusion.46, bf16[4096,512]{1,0:T(8,128)(2,1)} %all-gather.7.cloned.1.call-done, bf16[128,8,4,128]{3,2,1,0:T(4,128)(2,1)S(1)} %bitcast.198), kind=kOutput, calls=%fused_computation | convolution fusion | flops 4307550208 | bytes 47185920 | tf_op jit(solution)/shard_map/dot_general | solution.py:123
  558.7 30.3 %all_to_all.182 = bf16[4,256,512]{2,1,0:T(8,128)(2,1)S(1)} all-to-all(bf16[4,256,512]{2,1,0:T(8,128)(2,1)S(1)} %bitcast.218), channel_id=1, replica_groups=mesh['fa'=4,'fb'=4,'head'=2] {'fa'}, dimensions={0} | all-to-all | bytes 2097152 | tf_op jit(solution)/shard_map/all_to_all | solution.py:63
  589.0 28.8 %all_to_all.183 = bf16[4,256,512]{2,1,0:T(8,128)(2,1)S(1)} all-to-all(bf16[4,256,512]{2,1,0:T(8,128)(2,1)} %bitcast.219), channel_id=1, replica_groups=mesh['fa'=4,'fb'=4,'head'=2] {'fa'}, dimensions={0} | all-to-all | bytes 2097152 | tf_op jit(solution)/shard_map/all_to_all | solution.py:63
  617.8 3.5 all-to-all-start.13
  622.4 23.7 %all-to-all-done.13 = bf16[4,256,512]{2,1,0:T(8,128)(2,1)S(1)} async-done(((bf16[4,256,512]{2,1,0:T(8,128)(2,1)}), bf16[4,256,512]{2,1,0:T(8,128)(2,1)S(1)}, u32[]{:S(2)}, u32[]{:S(2)}) %all-to-all-start.13) | async-done | bytes 1048608 | tf_op jit(solution)/shard_map/all_to_all | solution.py:63
  650.8 6.3 reduce-scatter.12.cloned.1.call-done
  657.2 79.7 %reduce-scatter.14.cloned.1.call-done = bf16[256,2048]{1,0:T(8,128)(2,1)} async-done(((bf16[1024,2048]{1,0:T(8,128)(2,1)}), bf16[256,2048]{1,0:T(8,128)(2,1)}) %reduce-scatter.14.cloned.1.call-update) | async-done | bytes 1048592 | tf_op jit(solution)/shard_map/reduce_scatter | solution.py:131
  (156 shorter events, 114.3 us)
Async XLA Ops:
  7.2 193.6 %all-gather.5.cloned.1.call-start = ((), (), s32[]{:S(2)}) async-start(), calls=%async_computation.19 | async-start | bytes 10485760 | tf_op jit(solution)/shard_map/all_gather | solution.py:65
  7.9 9.2 %copy-start.14 = (bf16[256,2048]{1,0:T(8,128)(2,1)S(1)}, bf16[256,2048]{1,0:T(8,128)(2,1)}, u32[]{:S(2)}) copy-start(bf16[256,2048]{1,0:T(8,128)(2,1)} %param.8) | copy-start | bytes 3145732
  10.7 63.6 %copy-start.15 = (bf16[256,2048]{1,0:T(8,128)(2,1)S(1)}, bf16[256,2048]{1,0:T(8,128)(2,1)}, u32[]{:S(2)}) copy-start(bf16[256,2048]{1,0:T(8,128)(2,1)} %param.9) | copy-start | bytes 3145732
  10.7 60.0 %all-to-all-start = ((bf16[4,256,512]{1,2,0:T(8,128)(2,1)}), bf16[4,256,512]{1,2,0:T(8,128)(2,1)S(1)}, u32[]{:S(2)}, u32[]{:S(2)}) async-start(bf16[4,256,512]{1,2,0:T(8,128)(2,1)} %copy.104), calls=%async_computation | async-start | bytes 2097152 | tf_op jit(solution)/shard_map/all_to_all | solution.py:63
  70.7 57.9 %all-to-all-start.1 = ((bf16[4,256,512]{2,1,0:T(8,128)(2,1)}), bf16[4,256,512]{2,1,0:T(8,128)(2,1)S(1)}, u32[]{:S(2)}, u32[]{:S(2)}) async-start(bf16[4,256,512]{2,1,0:T(8,128)(2,1)} %bitcast.4), calls=%async_computation.1 | async-start | bytes 2097152 | tf_op jit(solution)/shard_map/all_to_all | solution.py:63
  74.2 205.3 %all-gather.9.cloned.1.call-start = ((), (), s32[]{:S(2)}) async-start(), calls=%async_computation.21 | async-start | bytes 5242880 | tf_op jit(solution)/shard_map/all_gather | solution.py:71
  128.6 72.2 %copy-start.5 = (bf16[4,256,512]{2,1,0:T(8,128)(2,1)}, bf16[4,256,512]{2,1,0:T(8,128)(2,1)S(1)}, u32[]{:S(2)}) copy-start(bf16[4,256,512]{2,1,0:T(8,128)(2,1)S(1)} %all-to-all-done.1) | copy-start | bytes 3145732
  200.8 102.6 %all-gather.11.cloned.1.call-start = ((), (), s32[]{:S(2)}) async-start(), calls=%async_computation.22 | async-start | bytes 5242880 | tf_op jit(solution)/shard_map/all_gather | solution.py:71
  231.4 28.8 %all-to-all-start.3 = ((bf16[4,256,512]{2,1,0:T(8,128)(2,1)}), bf16[4,256,512]{2,1,0:T(8,128)(2,1)S(1)}, u32[]{:S(2)}, u32[]{:S(2)}) async-start(bf16[4,256,512]{2,1,0:T(8,128)(2,1)} %bitcast.211), calls=%async_computation.3 | async-start | bytes 2097152 | tf_op jit(solution)/shard_map/all_to_all | solution.py:63
  260.2 3.6 copy-start.4
  260.2 38.6 %all-to-all-start.2 = ((bf16[8,128,4,128]{3,0,2,1:T(8,128)(2,1)}), bf16[8,128,4,128]{3,0,2,1:T(8,128)(2,1)S(1)}, u32[]{:S(2)}, u32[]{:S(2)}) async-start(bf16[8,128,4,128]{3,0,2,1:T(8,128)(2,1)} %copy.107), calls=%async_computation.2 | async-start | bytes 2097152 | tf_op jit(solution)/shard_map/all_to_all | solution.py:81
  263.7 64.9 %all-gather.7.cloned.1.call-start = ((), (), s32[]{:S(2)}) async-start(), calls=%async_computation.20 | async-start | bytes 5242880 | tf_op jit(solution)/shard_map/all_gather | solution.py:71
  287.8 7.6 %copy-start = (f32[1024,512]{0,1:T(8,128)}, f32[1024,512]{0,1:T(8,128)S(1)}, u32[]{:S(2)}) copy-start(f32[1024,512]{0,1:T(8,128)S(1)} %get-tuple-element.65) | copy-start | bytes 6291460
  289.1 6.4 copy-start.20
  298.8 25.6 %all-to-all-start.5 = ((bf16[8,128,4,128]{3,2,0,1:T(4,128)(2,1)}), bf16[8,128,4,128]{3,2,0,1:T(4,128)(2,1)}, u32[]{:S(2)}, u32[]{:S(2)}) async-start(bf16[8,128,4,128]{3,2,0,1:T(4,128)(2,1)} %multiply_convert_fusion.1), calls=%async_computation.5 | async-start | bytes 2097152 | tf_op jit(solution)/shard_map/all_to_all | solution.py:81
  312.8 6.4 copy-start.21
  324.4 19.0 %all-to-all-start.7 = ((bf16[8,128,4,128]{3,2,0,1:T(4,128)(2,1)}), bf16[8,128,4,128]{3,2,0,1:T(4,128)(2,1)}, u32[]{:S(2)}, u32[]{:S(2)}) async-start(bf16[8,128,4,128]{3,2,0,1:T(4,128)(2,1)} %multiply_convert_fusion), calls=%async_computation.7 | async-start | bytes 2097152 | tf_op jit(solution)/shard_map/all_to_all | solution.py:81
  343.4 19.3 %all-to-all-start.4 = ((bf16[8,128,4,128]{3,2,0,1:T(4,128)(2,1)}), bf16[8,128,4,128]{3,2,0,1:T(4,128)(2,1)}, u32[]{:S(2)}, u32[]{:S(2)}) async-start(bf16[8,128,4,128]{3,2,0,1:T(4,128)(2,1)} %copy.110), calls=%async_computation.4 | async-start | bytes 2097152 | tf_op jit(solution)/shard_map/all_to_all | solution.py:81
  349.8 2.0 copy-start.6
  351.9 4.0 copy-start.7
  362.7 2.8 copy-start.1
  362.7 2.8 copy-start.8
  365.4 1.3 copy-start.9
  368.3 18.8 %all-to-all-start.8 = ((bf16[32,32,4,128]{3,2,1,0:T(4,128)(2,1)}), bf16[32,32,4,128]{3,2,1,0:T(4,128)(2,1)}, u32[]{:S(2)}, u32[]{:S(2)}) async-start(bf16[32,32,4,128]{3,2,1,0:T(4,128)(2,1)} %copy.121), calls=%async_computation.8 | async-start | bytes 2097152 | tf_op jit(solution)/shard_map/all_to_all | solution.py:84
  372.6 184.9 %reduce-scatter.6.cloned.1.call-start = ((), (), s32[]{:S(2)}) async-start(), calls=%async_computation.23 | async-start | bytes 5242880 | tf_op jit(solution)/shard_map/reduce_scatter | solution.py:111
  388.8 2.1 copy-start.3
  398.6 1.0 copy-start.10
  409.4 148.2 %reduce-scatter.10.cloned.1.call-start = ((), (), s32[]{:S(2)}) async-start(), calls=%async_computation.25 | async-start | bytes 5242880 | tf_op jit(solution)/shard_map/reduce_scatter | solution.py:111
  444.4 19.6 %all-to-all-start.9 = ((bf16[32,32,4,128]{3,2,1,0:T(4,128)(2,1)}), bf16[32,32,4,128]{3,2,1,0:T(4,128)(2,1)}, u32[]{:S(2)}, u32[]{:S(2)}) async-start(bf16[32,32,4,128]{3,2,1,0:T(4,128)(2,1)} %copy.127), calls=%async_computation.9 | async-start | bytes 2097152 | tf_op jit(solution)/shard_map/all_to_all | solution.py:84
  448.6 108.9 %reduce-scatter.8.cloned.1.call-start = ((), (), s32[]{:S(2)}) async-start(), calls=%async_computation.24 | async-start | bytes 5242880 | tf_op jit(solution)/shard_map/reduce_scatter | solution.py:111
  473.3 3.0 copy-start.2
  476.8 1.0 copy-start.12
  487.5 1.2 copy-start.13
  487.5 11.8 %copy-start.11 = (bf16[1024,512]{0,1:T(8,128)(2,1)S(1)}, bf16[1024,512]{0,1:T(8,128)(2,1)}, u32[]{:S(2)}) copy-start(bf16[1024,512]{0,1:T(8,128)(2,1)} %copy-done.10) | copy-start | bytes 3145732
  487.5 169.6 %reduce-scatter.12.cloned.1.call-start = ((), (), s32[]{:S(2)}) async-start(), calls=%async_computation.26 | async-start | bytes 12582912 | tf_op jit(solution)/shard_map/reduce_scatter | solution.py:128
  488.7 10.6 %copy-start.22 = (bf16[4096,512]{1,0:T(8,128)(2,1)S(1)}, bf16[4096,512]{1,0:T(8,128)(2,1)}, u32[]{:S(2)}) copy-start(bf16[4096,512]{1,0:T(8,128)(2,1)} %all-gather.9.cloned.1.call-done) | copy-start | bytes 12582916
  557.5 1.2 copy-start.16
  617.8 28.3 %all-to-all-start.13 = ((bf16[4,256,512]{2,1,0:T(8,128)(2,1)}), bf16[4,256,512]{2,1,0:T(8,128)(2,1)S(1)}, u32[]{:S(2)}, u32[]{:S(2)}) async-start(bf16[4,256,512]{2,1,0:T(8,128)(2,1)} %bitcast.217), calls=%async_computation.17 | async-start | bytes 2097152 | tf_op jit(solution)/shard_map/all_to_all | solution.py:63
  621.3 115.6 %reduce-scatter.14.cloned.1.call-start = ((), (), s32[]{:S(2)}) async-start(), calls=%async_computation.27 | async-start | bytes 5242880 | tf_op jit(solution)/shard_map/reduce_scatter | solution.py:131
  622.3 26.9 %copy-start.17 = (bf16[256,512]{1,0:T(8,128)(2,1)S(1)}, bf16[256,512]{1,0:T(8,128)(2,1)}, u32[]{:S(2)}) copy-start(bf16[256,512]{1,0:T(8,128)(2,1)} %get-tuple-element.39) | copy-start | bytes 786436
  622.3 26.9 %copy-start.18 = (bf16[256,512]{1,0:T(8,128)(2,1)S(1)}, bf16[256,512]{1,0:T(8,128)(2,1)}, u32[]{:S(2)}) copy-start(bf16[256,512]{1,0:T(8,128)(2,1)} %get-tuple-element.40) | copy-start | bytes 786436
  622.3 26.9 %copy-start.19 = (bf16[256,512]{1,0:T(8,128)(2,1)S(1)}, bf16[256,512]{1,0:T(8,128)(2,1)}, u32[]{:S(2)}) copy-start(bf16[256,512]{1,0:T(8,128)(2,1)} %get-tuple-element.41) | copy-start | bytes 786436
Sparse Core Ops, SparseCore 0:
  9.5 191.1 all-gather.4
  202.9 33.5 all-gather.8
  238.1 38.5 all-gather.10
  278.1 43.1 all-gather.6
  409.5 45.4 reduce-scatter.5
  457.4 44.8 reduce-scatter.9
  504.8 44.5 reduce-scatter.7
  557.7 99.4 reduce-scatter.11
  660.0 76.7 reduce-scatter.13
